TPU v7x, 256 devices: a whole 4x4x8 slice. The times are simulated.
256 devices in a mesh: bead: 16 (over x, z_lo), slab: 8 (over y, z_hi), grp: 2 (over core).
Axes of the slice: x: 4, y: 4, z: 8 (z_hi: 2, z_lo: 4; z = z_hi * 4 + z_lo), core: 2. Of those that a mesh axis runs over, the one named last changes fastest.
Arguments:
- positions: float32 [64, 3, 65536], P('bead', None, ('slab', 'grp')), may hold values from -6 to 6
- momenta: float32 [64, 3, 65536], P('bead', None, ('slab', 'grp')), may hold values from -12 to 12
- force_old: float32 [64, 3, 65536], P('bead', None, ('slab', 'grp')), may hold values from -6 to 6
- noise: float32 [64, 3, 65536], P('bead', None, ('slab', 'grp')), may hold values from -6 to 6
- mass: float32 [65536], P(('slab', 'grp')), may hold values from 1 to 16
- pair_list: int32 [65536, 32], P(('slab', 'grp')), may hold values from 0 to 4351, as said below
- desc_w: bfloat16 [128, 1600], replicated, may hold values from -0.5 to 0.5
- hidden_one: bfloat16 [1600, 240], replicated, may hold values from -0.15625 to 0.15625
- hidden_two: bfloat16 [240, 240], replicated, may hold values from -0.375 to 0.375
- hidden_three: bfloat16 [240, 240], replicated, may hold values from -0.375 to 0.375
- out_w: bfloat16 [240, 3], replicated, may hold values from -0.375 to 0.375
Outputs:
- new_positions: float32 [64, 3, 65536], P('bead', None, ('slab', 'grp'))
- new_momenta: float32 [64, 3, 65536], P('bead', None, ('slab', 'grp'))
- force_new: float32 [64, 3, 65536], P('bead', None, ('slab', 'grp'))
Inputs may be any that keep to these rules, and one draw needn't show every extreme that they name: `pair_list`: for the atom with index li in its slab, every entry lies in li .. li + 256; entries past a count of 16 to 32 per atom name the atom itself, li + 128.
All inputs are finite; a program needn't handle non-finite values.
Results may differ from a plain program's by a relative error of at most 0.00096.
Values sent between devices are 32-bit elements; how exact they have to be, the bound alone decides.
A program may use at most 128 MiB of HBM per device.

v0:
```python
import math
import jax
import jax.numpy as jnp
from jax import lax
from jax.sharding import PartitionSpec as P

BEADS = 64
NC = 8
EDGE = 128
TIME_STEP = 0.1
CYCLE_FREQ = 5.0
CENTROID_FRICTION = 1.0
PAIR_STRENGTH = 0.5


def padded(shard, sides, width):
    for axis, dim in sides:
        count, length = (lax.axis_size(axis), shard.shape[dim])
        up = [(i, (i + 1) % count) for i in range(count)]
        down = [(j, i) for i, j in up]
        last = lax.slice_in_dim(shard, length - width, length, axis=dim)
        first = lax.slice_in_dim(shard, 0, width, axis=dim)
        before = lax.ppermute(last, axis, up)
        after = lax.ppermute(first, axis, down)
        shard = jnp.concatenate([before, shard, after], axis=dim)
    return shard


def cycle_tables(beads, contracted):
    index = jnp.arange(beads, dtype=jnp.float32)
    mode_int = jnp.arange(beads, dtype=jnp.int32)[None, :]
    angle = 2.0 * jnp.pi * index[:, None] * index[None, :] / beads
    half_mode = beads // 2
    root_one = 1.0 / jnp.sqrt(jnp.float32(beads))
    root_two = jnp.sqrt(2.0 / jnp.float32(beads))
    basis = jnp.where(
        mode_int == 0,
        root_one * jnp.ones_like(angle),
        jnp.where(
            mode_int < half_mode,
            root_two * jnp.cos(angle),
            jnp.where(mode_int == half_mode, root_one * jnp.cos(angle), root_two * jnp.sin(angle)),
        ),
    )
    freq = 2.0 * CYCLE_FREQ * jnp.sin(jnp.pi * index / beads)
    cindex = jnp.arange(contracted, dtype=jnp.float32)
    spacing = index[None, :] / beads - cindex[:, None] / contracted
    kernel = jnp.ones_like(spacing)
    for order in range(1, contracted // 2):
        kernel = kernel + 2.0 * jnp.cos(2.0 * jnp.pi * order * spacing)
    kernel = kernel + jnp.cos(jnp.pi * contracted * spacing)
    return (basis, freq, kernel / beads)


def free_drift(modes_q, modes_p, freq, masses):
    step = 0.5 * TIME_STEP
    rate = freq[:, None, None]
    moving = rate > 0.0
    safe = jnp.where(moving, rate, 1.0)
    cosine = jnp.cos(safe * step)
    sine = jnp.sin(safe * step)
    new_q = jnp.where(
        moving,
        cosine * modes_q + sine / (masses * safe) * modes_p,
        modes_q + step * modes_p / masses,
    )
    new_p = jnp.where(moving, cosine * modes_p - masses * safe * sine * modes_q, modes_p)
    return (new_q, new_p)


def thermostat(modes_p, noise, freq, masses):
    friction = jnp.where(freq > 0.0, 2.0 * freq, CENTROID_FRICTION)
    keep = jnp.exp(-friction * TIME_STEP)[:, None, None]
    return keep * modes_p + jnp.sqrt(masses) * jnp.sqrt(1.0 - keep * keep) * noise


def banded_take(extended, lists, start):
    copies = extended.shape[0]
    count, width = lists.shape
    block = math.gcd(count, 128)
    span = block + 2 * EDGE
    flat = extended.reshape(copies * 3, extended.shape[2])
    columns = jnp.arange(span, dtype=jnp.int32)[:, None]

    def one_block(number):
        first = start + number * block
        window = lax.dynamic_slice_in_dim(flat, first, span, 1)
        rows = lax.dynamic_slice_in_dim(lists, number * block, block, 0) - first
        selector = (rows.reshape(1, block * width) == columns).astype(jnp.float32)
        picked = jnp.dot(
            window, selector, precision=lax.Precision.HIGHEST, preferred_element_type=jnp.float32
        )
        return picked.reshape(copies, 3, block, width)

    pieces = lax.map(one_block, jnp.arange(count // block, dtype=jnp.int32))
    return jnp.transpose(pieces, (1, 2, 0, 3, 4)).reshape(copies, 3, count, width)


def contracted_forces(extended, lists, start, weights):
    desc_w, hidden_one, hidden_two, hidden_three, out_w = weights
    count = lists.shape[0]
    copies = extended.shape[0]
    near = banded_take(extended, lists, start)
    own = lax.dynamic_slice_in_dim(extended, start + EDGE, count, 2)[:, :, :, None]
    apart = near - own
    closeness = 1.0 / (1.0 + jnp.sum(apart * apart, axis=1))
    env = jnp.concatenate([apart, closeness[:, None]], axis=1)
    env = jnp.transpose(env, (0, 2, 3, 1)).reshape(copies * count, -1).astype(jnp.bfloat16)
    layer = jnp.tanh(jnp.dot(env, desc_w, preferred_element_type=jnp.float32)).astype(jnp.bfloat16)
    for matrix in (hidden_one, hidden_two, hidden_three):
        layer = jnp.tanh(jnp.dot(layer, matrix, preferred_element_type=jnp.float32)).astype(
            jnp.bfloat16
        )
    output = jnp.dot(layer, out_w, preferred_element_type=jnp.float32)
    return jnp.transpose(output.reshape(copies, count, 3), (0, 2, 1))


def pair_forces(extended, lists):
    count = lists.shape[0]
    near = banded_take(extended, lists, jnp.int32(0))
    own = extended[:, :, EDGE : EDGE + count][:, :, :, None]
    apart = near - own
    closeness = 1.0 / (1.0 + jnp.sum(apart * apart, axis=1, keepdims=True))
    return PAIR_STRENGTH * jnp.sum(apart * closeness, axis=3)


def slab_edges(field):
    return padded(field, ((("slab", "grp"), 2),), EDGE)


def body(
    positions,
    momenta,
    force_old,
    noise,
    mass,
    pair_list,
    desc_w,
    hidden_one,
    hidden_two,
    hidden_three,
    out_w,
):
    best = lax.Precision.HIGHEST
    beads_local = positions.shape[0]
    slab_atoms = positions.shape[2]
    groups = lax.axis_size("bead")
    block_rows = slab_atoms // groups
    place = lax.axis_index("bead")
    start = place * block_rows
    basis, freq, contract = cycle_tables(BEADS, NC)
    weights = (desc_w, hidden_one, hidden_two, hidden_three, out_w)
    ratio = BEADS / NC
    kicked = momenta + 0.5 * TIME_STEP * force_old
    gathered_q, gathered_p, mode_noise = (
        lax.all_to_all(positions, "bead", split_axis=2, concat_axis=0, tiled=True),
        lax.all_to_all(kicked, "bead", split_axis=2, concat_axis=0, tiled=True),
        lax.all_to_all(noise, "bead", split_axis=2, concat_axis=0, tiled=True),
    )
    masses = lax.dynamic_slice_in_dim(mass, start, block_rows, 0)[None, None, :]
    modes_q = jnp.einsum("bk,bxa->kxa", basis, gathered_q, precision=best)
    modes_p = jnp.einsum("bk,bxa->kxa", basis, gathered_p, precision=best)
    modes_q, modes_p = free_drift(modes_q, modes_p, freq, masses)
    modes_p = thermostat(modes_p, mode_noise, freq, masses)
    modes_q, modes_p = free_drift(modes_q, modes_p, freq, masses)
    block_q = jnp.einsum("bk,kxa->bxa", basis, modes_q, precision=best)
    block_p = jnp.einsum("bk,kxa->bxa", basis, modes_p, precision=best)
    row_lists = lax.dynamic_slice_in_dim(pair_list, start, block_rows, 0)
    local_contract = lax.dynamic_slice_in_dim(contract, place * beads_local, beads_local, 1)
    new_q, moved = (
        lax.all_to_all(block_q, "bead", split_axis=0, concat_axis=2, tiled=True),
        lax.all_to_all(block_p, "bead", split_axis=0, concat_axis=2, tiled=True),
    )
    bead_terms = jnp.einsum("cb,bxa->cxa", local_contract, new_q, precision=best)
    slab_contracted = lax.psum(bead_terms, "bead")
    neural = contracted_forces(slab_edges(slab_contracted), row_lists, start, weights)
    spread = ratio * jnp.einsum(
        "cb,cxa->bxa",
        local_contract,
        lax.all_gather(neural, "bead", axis=2, tiled=True),
        precision=best,
    )
    bead_extended = padded(new_q, ((("slab", "grp"), 2),), EDGE)
    pairs = pair_forces(bead_extended, pair_list)
    force_new = pairs + spread
    return (new_q, moved + 0.5 * TIME_STEP * force_new, force_new)


def solution(mesh):
    placed = (
        P("bead", None, ("slab", "grp")),
        P("bead", None, ("slab", "grp")),
        P("bead", None, ("slab", "grp")),
        P("bead", None, ("slab", "grp")),
        P(("slab", "grp")),
        P(("slab", "grp"), None),
        P(),
        P(),
        P(),
        P(),
        P(),
    )
    return jax.shard_map(
        body,
        mesh=mesh,
        in_specs=placed,
        out_specs=(
            P("bead", None, ("slab", "grp")),
            P("bead", None, ("slab", "grp")),
            P("bead", None, ("slab", "grp")),
        ),
        check_vma=False,
    )
```

profile of v0, /device:TPU:0, one launch (start us, length us, event | category | flops | bytes accessed | tf_op | source)
XLA Modules:
  0.0 457.1 jit_solution(15007762217400926848)
XLA Ops:
  7.2 6.7 %copy.125 = f32[4,3,4096]{0,1,2:T(4,128)} copy(f32[4,3,4096]{2,0,1:T(4,128)} %param.18) | data formatting | bytes 393216 | tf_op args[3]
  13.9 8.9 %reshape.263 = f32[16,1,3072]{2,1,0:T(1,128)} reshape(f32[4096,3,4]{2,1,0:T(4,128)} %bitcast.121) | data formatting | bytes 393216
  22.8 6.8 %all-to-all-start.2 = ((f32[16,1,3072]{2,1,0:T(1,128)}), f32[16,1,3072]{2,1,0:T(1,128)S(1)}, u32[]{:S(2)}, u32[]{:S(2)}) async-start(f32[16,1,3072]{2,1,0:T(1,128)} %reshape.263), calls=%async_computation.2 | async-start | bytes 393216 | tf_op jit(solution)/shard_map/all_to_all | solution.py:158
  29.8 6.0 %copy.119 = f32[4,3,4096]{0,1,2:T(4,128)} copy(f32[4,3,4096]{2,0,1:T(4,128)S(1)} %copy-done.5) | data formatting | bytes 393216 | tf_op args[0]
  35.7 8.9 %reshape.267 = f32[16,1,3072]{2,1,0:T(1,128)} reshape(f32[4096,3,4]{2,1,0:T(4,128)} %bitcast.122) | data formatting | bytes 393216
  44.9 7.5 %all-to-all-start = ((f32[16,1,3072]{2,1,0:T(1,128)}), f32[16,1,3072]{2,1,0:T(1,128)S(1)}, u32[]{:S(2)}, u32[]{:S(2)}) async-start(f32[16,1,3072]{2,1,0:T(1,128)} %reshape.267), calls=%async_computation | async-start | bytes 393216 | tf_op jit(solution)/shard_map/all_to_all | solution.py:156
  52.5 6.0 %copy.122 = f32[4,3,4096]{0,1,2:T(4,128)} copy(f32[4,3,4096]{2,0,1:T(4,128)S(1)} %multiply_add_fusion.2) | data formatting | bytes 393216 | tf_op jit(solution)/shard_map/add | solution.py:154
  58.4 8.9 %reshape.265 = f32[16,1,3072]{2,1,0:T(1,128)} reshape(f32[4096,3,4]{2,1,0:T(4,128)} %bitcast.117) | data formatting | bytes 393216
  67.5 8.0 %all-to-all-start.1 = ((f32[16,1,3072]{2,1,0:T(1,128)}), f32[16,1,3072]{2,1,0:T(1,128)S(1)}, u32[]{:S(2)}, u32[]{:S(2)}) async-start(f32[16,1,3072]{2,1,0:T(1,128)} %reshape.265), calls=%async_computation.1 | async-start | bytes 393216 | tf_op jit(solution)/shard_map/all_to_all | solution.py:157
  78.0 7.2 %reshape.264 = f32[4096,3,4]{2,1,0:T(4,128)} reshape(f32[16,3072]{1,0:T(8,128)S(1)} %reduce.3) | data formatting | bytes 393216
  85.2 6.5 %copy.126 = f32[4,3,16,256]{3,0,2,1:T(4,128)S(1)} copy(f32[4,3,16,256]{0,1,3,2:T(4,128)} %bitcast.118) | data formatting | bytes 393216 | tf_op jit(solution)/shard_map/all_to_all | solution.py:158
  92.9 7.2 %reshape.268 = f32[4096,3,4]{2,1,0:T(4,128)} reshape(f32[16,3072]{1,0:T(8,128)S(1)} %reduce.4) | data formatting | bytes 393216
  100.1 6.5 %copy.120 = f32[4,3,16,256]{3,0,2,1:T(4,128)S(1)} copy(f32[4,3,16,256]{0,1,3,2:T(4,128)} %bitcast.119) | data formatting | bytes 393216 | tf_op jit(solution)/shard_map/all_to_all | solution.py:156
  107.8 7.2 %reshape.266 = f32[4096,3,4]{2,1,0:T(4,128)} reshape(f32[16,3072]{1,0:T(8,128)S(1)} %reduce.5) | data formatting | bytes 393216
  115.0 6.6 %copy.123 = f32[4,3,16,256]{3,0,2,1:T(4,128)S(1)} copy(f32[4,3,16,256]{0,1,3,2:T(4,128)} %bitcast.120) | data formatting | bytes 393216 | tf_op jit(solution)/shard_map/all_to_all | solution.py:157
  124.3 7.6 %all-to-all-start.3 = ((f32[64,3,256]{2,1,0:T(4,128)}), f32[64,3,256]{2,1,0:T(4,128)S(1)}, u32[]{:S(2)}, u32[]{:S(2)}) async-start(f32[64,3,256]{2,1,0:T(4,128)} %copy.127), calls=%async_computation.3 | async-start | bytes 524288 | tf_op jit(solution)/shard_map/all_to_all | solution.py:171
  136.4 4.6 %all-to-all-done.3 = f32[64,3,256]{2,1,0:T(4,128)S(1)} async-done(((f32[64,3,256]{2,1,0:T(4,128)}), f32[64,3,256]{2,1,0:T(4,128)S(1)}, u32[]{:S(2)}, u32[]{:S(2)}) %all-to-all-start.3) | async-done | bytes 196640 | tf_op jit(solution)/shard_map/all_to_all | solution.py:171
  141.0 3.7 all-to-all-start.4
  145.0 3.4 collective-permute-start.1
  149.9 3.9 all-to-all-done.4
  154.5 3.0 collective-permute-done
  157.6 173.7 %while.22 = (s32[]{:T(128)}, f32[32,4,3,128,32]{4,3,2,1,0:T(8,128)}, s32[32]{0:T(128)S(1)}, f32[12,4352]{1,0:T(8,128)S(1)}, s32[4096,32]{1,0:T(8,128)}, /*index=...) while((s32[]{:T(128)}, f32[32,4,3,128,32]{4,3,2,1,0:T(8,128)}, s32[32]{0:T(128)S(1)}, ...), condition=%wide.region_1.2_spmd.clone, body=%wide.region_0.1_spmd.clone.sunk | while | flops 228069376 | bytes 1679568 | solution.py:95
  159.8 2.0 fusion.127
  165.2 2.0 fusion.127
  170.6 2.0 fusion.127
  176.1 2.0 fusion.127
  181.5 2.0 fusion.127
  186.9 2.0 fusion.127
  192.3 2.0 fusion.127
  241.2 2.0 fusion.127
  252.0 2.0 fusion.127
  279.2 2.0 fusion.127
  290.0 2.0 fusion.127
  295.4 2.0 fusion.127
  300.8 2.0 fusion.127
  306.2 2.0 fusion.127
  322.5 2.0 fusion.127
  331.2 14.3 %multiply_reduce_fusion.1 = f32[4,32,128,32]{3,2,0,1:T(8,128)} fusion(f32[32,4,3,128,32]{4,3,2,1,0:T(8,128)} %get-tuple-element.72, f32[4,3,32,128]{3,1,0,2:T(4,128)S(1)} %copy.135), kind=kLoop, calls=%fused_computation.18 | loop fusion | flops 4194304 | bytes 8585216 | tf_op jit(solution)/shard_map/reduce_sum | solution.py:123
  345.5 4.5 add_divide_fusion
  350.0 16.5 %multiply_reduce_fusion = f32[4,3,32,128]{3,1,0,2:T(4,128)S(1)} fusion(f32[32,4,3,128,32]{4,3,2,1,0:T(8,128)} %get-tuple-element.72, f32[4,32,128,32]{3,2,0,1:T(8,128)S(1)} %add_divide_fusion, f32[4,3,32,128]{3,1,0,2:T(4,128)S(1)} %copy.135), kind=kLoop, calls=%fused_computation.17 | loop fusion | flops 4669440 | bytes 8781824 | tf_op jit(solution)/shard_map/reduce_sum | solution.py:124
  367.4 8.0 %collective-permute-start.3 = (f32[8,3,128]{2,0,1:T(8,128)S(1)}, f32[8,3,128]{2,0,1:T(8,128)S(1)}, u32[]{:S(2)}, u32[]{:S(2)}) collective-permute-start(f32[8,3,128]{2,0,1:T(8,128)S(1)} %get-tuple-element.149), channel_id=1, source_target_pairs={{1,0},{2,1},{3,2},{4,3},{5,4},{6,5},{7,6},{8,7},{9,8},{10,9},{11,1... | collective-permute-start | bytes 36872 | tf_op jit(solution)/shard_map/ppermute | solution.py:24
  378.7 11.8 %while.23 = (s32[]{:T(128)}, f32[2,8,3,128,32]{4,3,2,1,0:T(8,128)}, s32[2]{0:T(128)S(1)}, s32[]{:T(128)}, f32[24,4352]{1,0:T(8,128)}, /*index=5*/s32[256,32]{1,0...) while((s32[]{:T(128)}, f32[2,8,3,128,32]{4,3,2,1,0:T(8,128)}, ...), condition=%wide.region_6.7_spmd.clone, body=%wide.region_5.6_spmd.clone.sunk | while | flops 454561792 | bytes 3264749 | solution.py:95
  380.1 2.8 fusion.129
  386.0 2.8 fusion.129
  390.6 2.5 multiply_reduce_fusion.2
  393.6 2.4 copy.141
  397.3 4.6 %fusion.15 = bf16[2048,240]{0,1:T(8,128)(2,1)S(1)} fusion(bf16[1600,240]{0,1:T(8,128)(2,1)S(1)} %copy-done, bf16[128,1600]{0,1:T(8,128)(2,1)} %param.21, bf16[2048,128]{0,1:T(8,128)(2,1)S(1)} %bitcast.138), kind=kOutput, calls=%fused_computation.28 | convolution fusion | flops 2415493120 | bytes 2684928 | tf_op jit(solution)/shard_map/dot_general | solution.py:111
  403.0 45.6 %all_gather.3 = f32[8,3,4096]{2,0,1:T(8,128)S(1)} all-gather(f32[8,3,256]{2,0,1:T(8,128)S(1)} %bitcast.140), channel_id=1, replica_groups=mesh['bead'=16,'slab'=8,'grp'=2] {'bead'}, dimensions={2}, use_global_device_ids=true | all-gather | bytes 417792 | tf_op jit(solution)/shard_map/all_gather | solution.py:180
  (291 shorter events, 150.8 us)
Async XLA Ops:
  7.2 390.1 %copy-start = (bf16[1600,240]{0,1:T(8,128)(2,1)S(1)}, bf16[1600,240]{0,1:T(8,128)(2,1)}, u32[]{:S(2)}) copy-start(bf16[1600,240]{0,1:T(8,128)(2,1)} %param.22) | copy-start | bytes 2304004
  7.2 22.4 %copy-start.3 = (f32[4,3,4096]{2,0,1:T(4,128)S(1)}, f32[4,3,4096]{2,0,1:T(4,128)}, u32[]{:S(2)}) copy-start(f32[4,3,4096]{2,0,1:T(4,128)} %param.16) | copy-start | bytes 589828
  7.2 22.4 %copy-start.4 = (f32[4,3,4096]{2,0,1:T(4,128)S(1)}, f32[4,3,4096]{2,0,1:T(4,128)}, u32[]{:S(2)}) copy-start(f32[4,3,4096]{2,0,1:T(4,128)} %param.17) | copy-start | bytes 589828
  7.2 22.6 %copy-start.5 = (f32[4,3,4096]{2,0,1:T(4,128)S(1)}, f32[4,3,4096]{2,0,1:T(4,128)}, u32[]{:S(2)}) copy-start(f32[4,3,4096]{2,0,1:T(4,128)} %param.15) | copy-start | bytes 589828
  22.8 22.1 %all-to-all-start.2 = ((f32[16,1,3072]{2,1,0:T(1,128)}), f32[16,1,3072]{2,1,0:T(1,128)S(1)}, u32[]{:S(2)}, u32[]{:S(2)}) async-start(f32[16,1,3072]{2,1,0:T(1,128)} %reshape.263), calls=%async_computation.2 | async-start | bytes 393216 | tf_op jit(solution)/shard_map/all_to_all | solution.py:158
  44.9 22.5 %all-to-all-start = ((f32[16,1,3072]{2,1,0:T(1,128)}), f32[16,1,3072]{2,1,0:T(1,128)S(1)}, u32[]{:S(2)}, u32[]{:S(2)}) async-start(f32[16,1,3072]{2,1,0:T(1,128)} %reshape.267), calls=%async_computation | async-start | bytes 393216 | tf_op jit(solution)/shard_map/all_to_all | solution.py:156
  67.5 39.2 %all-to-all-start.1 = ((f32[16,1,3072]{2,1,0:T(1,128)}), f32[16,1,3072]{2,1,0:T(1,128)S(1)}, u32[]{:S(2)}, u32[]{:S(2)}) async-start(f32[16,1,3072]{2,1,0:T(1,128)} %reshape.265), calls=%async_computation.1 | async-start | bytes 393216 | tf_op jit(solution)/shard_map/all_to_all | solution.py:157
  115.0 17.1 %copy-start.2 = (s32[4096,32]{0,1:T(8,128)S(1)}, s32[4096,32]{0,1:T(8,128)}, u32[]{:S(2)}) copy-start(s32[4096,32]{0,1:T(8,128)} %param.20) | copy-start | bytes 1572868
  124.3 16.7 %all-to-all-start.3 = ((f32[64,3,256]{2,1,0:T(4,128)}), f32[64,3,256]{2,1,0:T(4,128)S(1)}, u32[]{:S(2)}, u32[]{:S(2)}) async-start(f32[64,3,256]{2,1,0:T(4,128)} %copy.127), calls=%async_computation.3 | async-start | bytes 524288 | tf_op jit(solution)/shard_map/all_to_all | solution.py:171
  141.0 12.8 %all-to-all-start.4 = ((f32[64,3,256]{2,1,0:T(4,128)}), f32[64,3,256]{2,1,0:T(4,128)S(1)}, u32[]{:S(2)}, u32[]{:S(2)}) async-start(f32[64,3,256]{2,1,0:T(4,128)} %copy.130), calls=%async_computation.4 | async-start | bytes 524288 | tf_op jit(solution)/shard_map/all_to_all | solution.py:172
  144.7 221.8 %all-reduce.2.cloned.1.call-start = ((), (), s32[]{:S(2)}) async-start(), calls=%async_computation.5 | async-start | bytes 786432 | tf_op jit(solution)/shard_map/psum | solution.py:175
  145.0 12.5 %copy-start.1 = (f32[4,3,4096]{2,0,1:T(4,128)}, f32[4,3,4096]{2,0,1:T(4,128)S(1)}, u32[]{:S(2)}) copy-start(f32[4,3,4096]{2,0,1:T(4,128)S(1)} %all_to_all.80) | copy-start | bytes 589828
  145.0 9.4 %collective-permute-start.1 = (f32[4,3,128]{2,0,1:T(4,128)S(1)}, f32[4,3,128]{2,0,1:T(4,128)S(1)}, u32[]{:S(2)}, u32[]{:S(2)}) collective-permute-start(f32[4,3,128]{2,0,1:T(4,128)S(1)} %get-tuple-element.152), channel_id=1, source_target_pairs={{1,0},{2,1},{3,2},{4,3},{5,4},{6,5},{7,6},{8,7},{9,8},{10,9},{11,1... | collective-permute-start | bytes 18440 | tf_op jit(solution)/shard_map/ppermute | solution.py:24
  148.4 9.1 %collective-permute-start = (f32[4,3,128]{2,0,1:T(4,128)S(1)}, f32[4,3,128]{2,0,1:T(4,128)S(1)}, u32[]{:S(2)}, u32[]{:S(2)}) collective-permute-start(f32[4,3,128]{2,0,1:T(4,128)S(1)} %get-tuple-element.151), channel_id=1, source_target_pairs={{0,1},{1,2},{2,3},{3,4},{4,5},{5,6},{6,7},{7,8},{8,9},{9,10},{10,1... | collective-permute-start | bytes 18440 | tf_op jit(solution)/shard_map/ppermute | solution.py:23
  367.2 9.1 %collective-permute-start.2 = (f32[8,3,128]{2,0,1:T(8,128)S(1)}, f32[8,3,128]{2,0,1:T(8,128)S(1)}, u32[]{:S(2)}, u32[]{:S(2)}) collective-permute-start(f32[8,3,128]{2,0,1:T(8,128)S(1)} %get-tuple-element.150), channel_id=1, source_target_pairs={{0,1},{1,2},{2,3},{3,4},{4,5},{5,6},{6,7},{7,8},{8,9},{9,10},{10,1... | collective-permute-start | bytes 36872 | tf_op jit(solution)/shard_map/ppermute | solution.py:23
  367.4 10.0 %collective-permute-start.3 = (f32[8,3,128]{2,0,1:T(8,128)S(1)}, f32[8,3,128]{2,0,1:T(8,128)S(1)}, u32[]{:S(2)}, u32[]{:S(2)}) collective-permute-start(f32[8,3,128]{2,0,1:T(8,128)S(1)} %get-tuple-element.149), channel_id=1, source_target_pairs={{1,0},{2,1},{3,2},{4,3},{5,4},{6,5},{7,6},{8,7},{9,8},{10,9},{11,1... | collective-permute-start | bytes 36872 | tf_op jit(solution)/shard_map/ppermute | solution.py:24
  396.0 5.9 %copy-start.6 = (bf16[240,240]{1,0:T(8,128)(2,1)S(1)}, bf16[240,240]{1,0:T(8,128)(2,1)}, u32[]{:S(2)}) copy-start(bf16[240,240]{1,0:T(8,128)(2,1)} %param.23) | copy-start | bytes 345604
  396.8 5.6 %copy-start.7 = (bf16[240,240]{1,0:T(8,128)(2,1)S(1)}, bf16[240,240]{1,0:T(8,128)(2,1)}, u32[]{:S(2)}) copy-start(bf16[240,240]{1,0:T(8,128)(2,1)} %param.24) | copy-start | bytes 345604
  396.8 5.6 %copy-start.8 = (bf16[240,3]{0,1:T(4,128)(2,1)S(1)}, bf16[240,3]{0,1:T(4,128)(2,1)}, u32[]{:S(2)}) copy-start(bf16[240,3]{0,1:T(4,128)(2,1)} %param.25) | copy-start | bytes 4324
Sparse Core Ops, SparseCore 0:
  154.6 160.6 all-reduce.1
where the time goes:
time: 464 us; the launch traced here: 457 us
  local copies, waits for them, and re-layouts  167 us (36%)
  matrix products  81.2 us (18%)
  other arithmetic  69.4 us (15%)
  blocking collectives  45.6 us (10%)
  starting transfers between devices  45 us (10%)
  loops' own time  21.9 us (5%)
  between operations  14.9 us (3%)
  waiting for transfers between devices  12.5 us (3%)
    dot_general x34, matrix products, one_block(): jnp.dot(window, selector, precision=lax.Precision.HIGHEST, preferred_elem...  70.5 us
    unnamed x33, local copies, waits for them, and re-layouts  64.3 us
    all_gather x1, blocking collectives, body(): lax.all_gather(neural, 'bead', axis=2, tiled=True)  45.6 us
    dynamic_update_slice x34, local copies, waits for them, and re-layouts, banded_take(): pieces = lax.map(one_block, jnp.arange(count // block, dtype=jnp.int32))  33.3 us
    sub x34, other arithmetic, one_block(): rows = lax.dynamic_slice_in_dim(lists, number * block, block, 0) - first  27.3 us
    another operation x2, loops' own time, banded_take(): pieces = lax.map(one_block, jnp.arange(count // block, dtype=jnp.int32))  21.9 us
    dynamic_slice x34, local copies, waits for them, and re-layouts, banded_take(): pieces = lax.map(one_block, jnp.arange(count // block, dtype=jnp.int32))  21.5 us
    reduce_sum x1, other arithmetic, pair_forces(): return PAIR_STRENGTH * jnp.sum(apart * closeness, axis=3)  16.5 us
  transfers between devices with their start and end apart: 10, of which 4 were waited for; matrix products, arithmetic and copies ran while one was open for 56% of the time, Pallas kernels for 0%

commit v1 on v0

--- a/solution.py
+++ b/solution.py
@@ -11,6 +11,11 @@
 CYCLE_FREQ = 5.0
 CENTROID_FRICTION = 1.0
 PAIR_STRENGTH = 0.5
+
+
+def all_by_exchange(x, mesh_axis, dim):
+    sent = jnp.stack([x] * lax.axis_size(mesh_axis))
+    return jnp.concatenate(lax.all_to_all(sent, mesh_axis, 0, 0), axis=dim)
 
 
 def padded(shard, sides, width):
@@ -175,10 +180,7 @@
     slab_contracted = lax.psum(bead_terms, "bead")
     neural = contracted_forces(slab_edges(slab_contracted), row_lists, start, weights)
     spread = ratio * jnp.einsum(
-        "cb,cxa->bxa",
-        local_contract,
-        lax.all_gather(neural, "bead", axis=2, tiled=True),
-        precision=best,
+        "cb,cxa->bxa", local_contract, all_by_exchange(neural, "bead", 2), precision=best
     )
     bead_extended = padded(new_q, ((("slab", "grp"), 2),), EDGE)
     pairs = pair_forces(bead_extended, pair_list)

time: 464 us -> 434 us (0.935)
  the two profiles are of different devices: /device:TPU:0 before, /device:TPU:2 now
where the time goes in v1:
time: 434 us; the launch traced here: 427 us
  local copies, waits for them, and re-layouts  165 us (38%)
  matrix products  82.1 us (19%)
  other arithmetic  74.4 us (17%)
  starting transfers between devices  56.3 us (13%)
  loops' own time  22.3 us (5%)
  between operations  14.8 us (3%)
  waiting for transfers between devices  11.4 us (3%)
    dot_general x34, matrix products, one_block(): jnp.dot(window, selector, precision=lax.Precision.HIGHEST, preferred_elem...  70.5 us
    unnamed x33, local copies, waits for them, and re-layouts  63.4 us
    dynamic_update_slice x34, local copies, waits for them, and re-layouts, banded_take(): pieces = lax.map(one_block, jnp.arange(count // block, dtype=jnp.int32))  33.2 us
    sub x34, other arithmetic, one_block(): rows = lax.dynamic_slice_in_dim(lists, number * block, block, 0) - first  27.2 us
    another operation x2, loops' own time, banded_take(): pieces = lax.map(one_block, jnp.arange(count // block, dtype=jnp.int32))  22.3 us
    dynamic_slice x34, local copies, waits for them, and re-layouts, banded_take(): pieces = lax.map(one_block, jnp.arange(count // block, dtype=jnp.int32))  20.5 us
    reduce_sum x1, other arithmetic, pair_forces(): return PAIR_STRENGTH * jnp.sum(apart * closeness, axis=3)  17.5 us
    reduce_sum x1, other arithmetic, pair_forces(): closeness = 1.0 / (1.0 + jnp.sum(apart * apart, axis=1, keepdims=True))  14.3 us
  transfers between devices with their start and end apart: 11, of which 4 were waited for; matrix products, arithmetic and copies ran while one was open for 61% of the time, Pallas kernels for 0%

profile of v1, /device:TPU:2, one launch (start us, length us, event | category | flops | bytes accessed | tf_op | source)
XLA Modules:
  0.0 426.7 jit_solution(16472265749140795430)
XLA Ops:
  7.2 6.7 %copy.128 = f32[4,3,4096]{0,1,2:T(4,128)} copy(f32[4,3,4096]{2,0,1:T(4,128)} %param.18) | data formatting | bytes 393216 | tf_op args[3]
  13.9 8.9 %reshape.273 = f32[16,1,3072]{2,1,0:T(1,128)} reshape(f32[4096,3,4]{2,1,0:T(4,128)} %bitcast.123) | data formatting | bytes 393216
  22.9 8.9 %all-to-all-start.2 = ((f32[16,1,3072]{2,1,0:T(1,128)}), f32[16,1,3072]{2,1,0:T(1,128)S(1)}, u32[]{:S(2)}, u32[]{:S(2)}) async-start(f32[16,1,3072]{2,1,0:T(1,128)} %reshape.273), calls=%async_computation.2 | async-start | bytes 393216 | tf_op jit(solution)/shard_map/all_to_all | solution.py:163
  31.9 6.0 %copy.122 = f32[4,3,4096]{0,1,2:T(4,128)} copy(f32[4,3,4096]{2,0,1:T(4,128)S(1)} %copy-done.6) | data formatting | bytes 393216 | tf_op args[0]
  37.9 8.9 %reshape.277 = f32[16,1,3072]{2,1,0:T(1,128)} reshape(f32[4096,3,4]{2,1,0:T(4,128)} %bitcast.124) | data formatting | bytes 393216
  47.1 7.5 %all-to-all-start = ((f32[16,1,3072]{2,1,0:T(1,128)}), f32[16,1,3072]{2,1,0:T(1,128)S(1)}, u32[]{:S(2)}, u32[]{:S(2)}) async-start(f32[16,1,3072]{2,1,0:T(1,128)} %reshape.277), calls=%async_computation | async-start | bytes 393216 | tf_op jit(solution)/shard_map/all_to_all | solution.py:161
  54.6 6.0 %copy.125 = f32[4,3,4096]{0,1,2:T(4,128)} copy(f32[4,3,4096]{2,0,1:T(4,128)S(1)} %multiply_add_fusion.2) | data formatting | bytes 393216 | tf_op jit(solution)/shard_map/add | solution.py:159
  60.6 8.9 %reshape.275 = f32[16,1,3072]{2,1,0:T(1,128)} reshape(f32[4096,3,4]{2,1,0:T(4,128)} %bitcast.119) | data formatting | bytes 393216
  69.7 7.9 %all-to-all-start.1 = ((f32[16,1,3072]{2,1,0:T(1,128)}), f32[16,1,3072]{2,1,0:T(1,128)S(1)}, u32[]{:S(2)}, u32[]{:S(2)}) async-start(f32[16,1,3072]{2,1,0:T(1,128)} %reshape.275), calls=%async_computation.1 | async-start | bytes 393216 | tf_op jit(solution)/shard_map/all_to_all | solution.py:162
  80.1 7.2 %reshape.274 = f32[4096,3,4]{2,1,0:T(4,128)} reshape(f32[16,3072]{1,0:T(8,128)S(1)} %reduce.3) | data formatting | bytes 393216
  87.3 6.5 %copy.129 = f32[4,3,16,256]{3,0,2,1:T(4,128)S(1)} copy(f32[4,3,16,256]{0,1,3,2:T(4,128)} %bitcast.120) | data formatting | bytes 393216 | tf_op jit(solution)/shard_map/all_to_all | solution.py:163
  95.0 7.2 %reshape.278 = f32[4096,3,4]{2,1,0:T(4,128)} reshape(f32[16,3072]{1,0:T(8,128)S(1)} %reduce.4) | data formatting | bytes 393216
  102.2 6.5 %copy.123 = f32[4,3,16,256]{3,0,2,1:T(4,128)S(1)} copy(f32[4,3,16,256]{0,1,3,2:T(4,128)} %bitcast.121) | data formatting | bytes 393216 | tf_op jit(solution)/shard_map/all_to_all | solution.py:161
  109.9 7.2 %reshape.276 = f32[4096,3,4]{2,1,0:T(4,128)} reshape(f32[16,3072]{1,0:T(8,128)S(1)} %reduce.5) | data formatting | bytes 393216
  117.1 6.6 %copy.126 = f32[4,3,16,256]{3,0,2,1:T(4,128)S(1)} copy(f32[4,3,16,256]{0,1,3,2:T(4,128)} %bitcast.122) | data formatting | bytes 393216 | tf_op jit(solution)/shard_map/all_to_all | solution.py:162
  126.4 7.5 %all-to-all-start.3 = ((f32[64,3,256]{2,1,0:T(4,128)}), f32[64,3,256]{2,1,0:T(4,128)S(1)}, u32[]{:S(2)}, u32[]{:S(2)}) async-start(f32[64,3,256]{2,1,0:T(4,128)} %copy.130), calls=%async_computation.3 | async-start | bytes 524288 | tf_op jit(solution)/shard_map/all_to_all | solution.py:176
  138.4 3.1 all-to-all-done.3
  141.5 5.5 %all-to-all-start.4 = ((f32[64,3,256]{2,1,0:T(4,128)}), f32[64,3,256]{2,1,0:T(4,128)S(1)}, u32[]{:S(2)}, u32[]{:S(2)}) async-start(f32[64,3,256]{2,1,0:T(4,128)} %copy.133), calls=%async_computation.4 | async-start | bytes 524288 | tf_op jit(solution)/shard_map/all_to_all | solution.py:177
  147.3 3.1 collective-permute-start.1
  152.0 2.7 all-to-all-done.4
  155.3 4.2 collective-permute-done
  159.6 172.9 %while.22 = (s32[]{:T(128)}, f32[32,4,3,128,32]{4,3,2,1,0:T(8,128)}, s32[32]{0:T(128)S(1)}, f32[12,4352]{1,0:T(8,128)S(1)}, s32[4096,32]{1,0:T(8,128)}, /*index=...) while((s32[]{:T(128)}, f32[32,4,3,128,32]{4,3,2,1,0:T(8,128)}, s32[32]{0:T(128)S(1)}, ...), condition=%wide.region_1.2_spmd.clone, body=%wide.region_0.1_spmd.clone.sunk | while | flops 228069376 | bytes 1679568 | solution.py:100
  161.8 2.0 fusion.127
  167.2 2.0 fusion.127
  172.6 2.0 fusion.127
  178.0 2.0 fusion.127
  183.3 2.0 fusion.127
  188.7 2.0 fusion.127
  194.1 2.0 fusion.127
  199.6 2.0 fusion.127
  205.0 2.0 fusion.127
  210.4 2.0 fusion.127
  221.2 2.0 fusion.127
  259.1 2.0 fusion.127
  275.3 2.0 fusion.127
  286.1 2.0 fusion.127
  296.9 2.0 fusion.127
  332.5 14.3 %multiply_reduce_fusion.1 = f32[4,32,128,32]{3,2,0,1:T(8,128)} fusion(f32[32,4,3,128,32]{4,3,2,1,0:T(8,128)} %get-tuple-element.72, f32[4,3,32,128]{3,1,0,2:T(4,128)S(1)} %copy.138), kind=kLoop, calls=%fused_computation.18 | loop fusion | flops 4194304 | bytes 8585216 | tf_op jit(solution)/shard_map/reduce_sum | solution.py:128
  347.5 8.5 %add_divide_fusion = f32[4,32,128,32]{3,2,0,1:T(8,128)} fusion(f32[4,32,128,32]{3,2,0,1:T(8,128)} %multiply_reduce_fusion.1), kind=kLoop, calls=%fused_computation.20 | loop fusion | flops 1048576 | bytes 4194304 | tf_op jit(solution)/shard_map/div | solution.py:128
  356.0 7.9 %collective-permute-start.3 = (f32[8,3,128]{2,0,1:T(8,128)S(1)}, f32[8,3,128]{2,0,1:T(8,128)S(1)}, u32[]{:S(2)}, u32[]{:S(2)}) collective-permute-start(f32[8,3,128]{2,0,1:T(8,128)S(1)} %get-tuple-element.149), channel_id=1, source_target_pairs={{1,0},{2,1},{3,2},{4,3},{5,4},{6,5},{7,6},{8,7},{9,8},{10,9},{11,1... | collective-permute-start | bytes 36872 | tf_op jit(solution)/shard_map/ppermute | solution.py:29
  366.6 11.8 %while.23 = (s32[]{:T(128)}, f32[2,8,3,128,32]{4,3,2,1,0:T(8,128)}, s32[2]{0:T(128)S(1)}, s32[]{:T(128)}, f32[24,4352]{1,0:T(8,128)}, /*index=5*/s32[256,32]{1,0...) while((s32[]{:T(128)}, f32[2,8,3,128,32]{4,3,2,1,0:T(8,128)}, ...), condition=%wide.region_6.7_spmd.clone, body=%wide.region_5.6_spmd.clone.sunk | while | flops 454561792 | bytes 3264749 | solution.py:100
  367.9 2.8 fusion.129
  373.8 2.8 fusion.129
  378.4 2.5 multiply_reduce_fusion.2
  381.5 2.4 copy.144
  385.1 4.6 %fusion.15 = bf16[2048,240]{0,1:T(8,128)(2,1)S(1)} fusion(bf16[1600,240]{0,1:T(8,128)(2,1)S(1)} %copy-done, bf16[128,1600]{0,1:T(8,128)(2,1)} %param.21, bf16[2048,128]{0,1:T(8,128)(2,1)S(1)} %bitcast.142), kind=kOutput, calls=%fused_computation.28 | convolution fusion | flops 2415493120 | bytes 2684928 | tf_op jit(solution)/shard_map/dot_general | solution.py:116
  392.6 7.9 %all-to-all-start.5 = ((f32[16,8,3,256]{3,1,2,0:T(8,128)}), f32[16,8,3,256]{3,1,2,0:T(8,128)S(1)}, u32[]{:S(2)}, u32[]{:S(2)}) async-start(f32[16,8,3,256]{3,1,2,0:T(8,128)} %stack.2), calls=%async_computation.5 | async-start | bytes 786432 | tf_op jit(solution)/shard_map/all_to_all | solution.py:18
  400.4 17.5 %multiply_reduce_fusion = f32[4,3,32,128]{3,1,0,2:T(4,128)S(1)} fusion(f32[32,4,3,128,32]{4,3,2,1,0:T(8,128)} %get-tuple-element.72, f32[4,32,128,32]{3,2,0,1:T(8,128)} %add_divide_fusion, f32[4,3,32,128]{3,1,0,2:T(4,128)S(1)} %copy.138), kind=kLoop, calls=%fused_computation.17 | loop fusion | flops 4669440 | bytes 8781824 | tf_op jit(solution)/shard_map/reduce_sum | solution.py:129
  (294 shorter events, 150.9 us)
Async XLA Ops:
  7.2 378.0 %copy-start = (bf16[1600,240]{0,1:T(8,128)(2,1)S(1)}, bf16[1600,240]{0,1:T(8,128)(2,1)}, u32[]{:S(2)}) copy-start(bf16[1600,240]{0,1:T(8,128)(2,1)} %param.22) | copy-start | bytes 2304004
  7.2 24.6 %copy-start.4 = (f32[4,3,4096]{2,0,1:T(4,128)S(1)}, f32[4,3,4096]{2,0,1:T(4,128)}, u32[]{:S(2)}) copy-start(f32[4,3,4096]{2,0,1:T(4,128)} %param.16) | copy-start | bytes 589828
  7.2 24.6 %copy-start.5 = (f32[4,3,4096]{2,0,1:T(4,128)S(1)}, f32[4,3,4096]{2,0,1:T(4,128)}, u32[]{:S(2)}) copy-start(f32[4,3,4096]{2,0,1:T(4,128)} %param.17) | copy-start | bytes 589828
  7.2 24.7 %copy-start.6 = (f32[4,3,4096]{2,0,1:T(4,128)S(1)}, f32[4,3,4096]{2,0,1:T(4,128)}, u32[]{:S(2)}) copy-start(f32[4,3,4096]{2,0,1:T(4,128)} %param.15) | copy-start | bytes 589828
  22.9 24.2 %all-to-all-start.2 = ((f32[16,1,3072]{2,1,0:T(1,128)}), f32[16,1,3072]{2,1,0:T(1,128)S(1)}, u32[]{:S(2)}, u32[]{:S(2)}) async-start(f32[16,1,3072]{2,1,0:T(1,128)} %reshape.273), calls=%async_computation.2 | async-start | bytes 393216 | tf_op jit(solution)/shard_map/all_to_all | solution.py:163
  47.1 22.6 %all-to-all-start = ((f32[16,1,3072]{2,1,0:T(1,128)}), f32[16,1,3072]{2,1,0:T(1,128)S(1)}, u32[]{:S(2)}, u32[]{:S(2)}) async-start(f32[16,1,3072]{2,1,0:T(1,128)} %reshape.277), calls=%async_computation | async-start | bytes 393216 | tf_op jit(solution)/shard_map/all_to_all | solution.py:161
  69.7 39.1 %all-to-all-start.1 = ((f32[16,1,3072]{2,1,0:T(1,128)}), f32[16,1,3072]{2,1,0:T(1,128)S(1)}, u32[]{:S(2)}, u32[]{:S(2)}) async-start(f32[16,1,3072]{2,1,0:T(1,128)} %reshape.275), calls=%async_computation.1 | async-start | bytes 393216 | tf_op jit(solution)/shard_map/all_to_all | solution.py:162
  117.1 17.0 %copy-start.2 = (s32[4096,32]{0,1:T(8,128)S(1)}, s32[4096,32]{0,1:T(8,128)}, u32[]{:S(2)}) copy-start(s32[4096,32]{0,1:T(8,128)} %param.20) | copy-start | bytes 1572868
  126.4 15.1 %all-to-all-start.3 = ((f32[64,3,256]{2,1,0:T(4,128)}), f32[64,3,256]{2,1,0:T(4,128)S(1)}, u32[]{:S(2)}, u32[]{:S(2)}) async-start(f32[64,3,256]{2,1,0:T(4,128)} %copy.130), calls=%async_computation.3 | async-start | bytes 524288 | tf_op jit(solution)/shard_map/all_to_all | solution.py:176
  141.5 13.2 %all-to-all-start.4 = ((f32[64,3,256]{2,1,0:T(4,128)}), f32[64,3,256]{2,1,0:T(4,128)S(1)}, u32[]{:S(2)}, u32[]{:S(2)}) async-start(f32[64,3,256]{2,1,0:T(4,128)} %copy.133), calls=%async_computation.4 | async-start | bytes 524288 | tf_op jit(solution)/shard_map/all_to_all | solution.py:177
  147.0 199.7 %all-reduce.2.cloned.1.call-start = ((), (), s32[]{:S(2)}) async-start(), calls=%async_computation.6 | async-start | bytes 786432 | tf_op jit(solution)/shard_map/psum | solution.py:180
  147.3 12.3 %copy-start.1 = (f32[4,3,4096]{2,0,1:T(4,128)}, f32[4,3,4096]{2,0,1:T(4,128)S(1)}, u32[]{:S(2)}) copy-start(f32[4,3,4096]{2,0,1:T(4,128)S(1)} %all_to_all.83) | copy-start | bytes 589828
  147.3 8.0 %collective-permute-start.1 = (f32[4,3,128]{2,0,1:T(4,128)S(1)}, f32[4,3,128]{2,0,1:T(4,128)S(1)}, u32[]{:S(2)}, u32[]{:S(2)}) collective-permute-start(f32[4,3,128]{2,0,1:T(4,128)S(1)} %get-tuple-element.152), channel_id=1, source_target_pairs={{1,0},{2,1},{3,2},{4,3},{5,4},{6,5},{7,6},{8,7},{9,8},{10,9},{11,1... | collective-permute-start | bytes 18440 | tf_op jit(solution)/shard_map/ppermute | solution.py:29
  150.4 9.1 %collective-permute-start = (f32[4,3,128]{2,0,1:T(4,128)S(1)}, f32[4,3,128]{2,0,1:T(4,128)S(1)}, u32[]{:S(2)}, u32[]{:S(2)}) collective-permute-start(f32[4,3,128]{2,0,1:T(4,128)S(1)} %get-tuple-element.151), channel_id=1, source_target_pairs={{0,1},{1,2},{2,3},{3,4},{4,5},{5,6},{6,7},{7,8},{8,9},{9,10},{10,1... | collective-permute-start | bytes 18440 | tf_op jit(solution)/shard_map/ppermute | solution.py:28
  347.5 16.3 %copy-start.3 = (f32[8,3,4096]{2,0,1:T(8,128)S(1)}, f32[8,3,4096]{2,0,1:T(8,128)}, u32[]{:S(2)}) copy-start(f32[8,3,4096]{2,0,1:T(8,128)} %all-reduce.2.cloned.1.call-done) | copy-start | bytes 1179652
  347.5 16.3 %collective-permute-start.2 = (f32[8,3,128]{2,0,1:T(8,128)S(1)}, f32[8,3,128]{2,0,1:T(8,128)S(1)}, u32[]{:S(2)}, u32[]{:S(2)}) collective-permute-start(f32[8,3,128]{2,0,1:T(8,128)S(1)} %get-tuple-element.150), channel_id=1, source_target_pairs={{0,1},{1,2},{2,3},{3,4},{4,5},{5,6},{6,7},{7,8},{8,9},{9,10},{10,1... | collective-permute-start | bytes 36872 | tf_op jit(solution)/shard_map/ppermute | solution.py:28
  356.0 9.3 %collective-permute-start.3 = (f32[8,3,128]{2,0,1:T(8,128)S(1)}, f32[8,3,128]{2,0,1:T(8,128)S(1)}, u32[]{:S(2)}, u32[]{:S(2)}) collective-permute-start(f32[8,3,128]{2,0,1:T(8,128)S(1)} %get-tuple-element.149), channel_id=1, source_target_pairs={{1,0},{2,1},{3,2},{4,3},{5,4},{6,5},{7,6},{8,7},{9,8},{10,9},{11,1... | collective-permute-start | bytes 36872 | tf_op jit(solution)/shard_map/ppermute | solution.py:29
  383.9 5.9 %copy-start.7 = (bf16[240,240]{1,0:T(8,128)(2,1)S(1)}, bf16[240,240]{1,0:T(8,128)(2,1)}, u32[]{:S(2)}) copy-start(bf16[240,240]{1,0:T(8,128)(2,1)} %param.23) | copy-start | bytes 345604
  384.6 5.6 %copy-start.8 = (bf16[240,3]{0,1:T(4,128)(2,1)S(1)}, bf16[240,3]{0,1:T(4,128)(2,1)}, u32[]{:S(2)}) copy-start(bf16[240,3]{0,1:T(4,128)(2,1)} %param.25) | copy-start | bytes 4324
  392.6 25.6 %all-to-all-start.5 = ((f32[16,8,3,256]{3,1,2,0:T(8,128)}), f32[16,8,3,256]{3,1,2,0:T(8,128)S(1)}, u32[]{:S(2)}, u32[]{:S(2)}) async-start(f32[16,8,3,256]{3,1,2,0:T(8,128)} %stack.2), calls=%async_computation.5 | async-start | bytes 786432 | tf_op jit(solution)/shard_map/all_to_all | solution.py:18
Sparse Core Ops, SparseCore 0:
  155.4 156.0 all-reduce.1
